TPU v7x, 512 devices: a whole 4x8x8 slice. The times are simulated.
512 devices in a mesh: seq: 64 (over x, y, core), chan: 8 (over z).
Axes of the slice: x: 4, y: 8, z: 8, core: 2. Of those that a mesh axis runs over, the one named last changes fastest.
Arguments:
- gate_outer: bfloat16 [8192, 4096], P('seq', 'chan'), may hold values from -520 to 520
- gate_inner: bfloat16 [8192, 4096], P('seq', 'chan'), may hold values from -6 to 6
- value_in: bfloat16 [8192, 4096], P('seq', 'chan'), may hold values from -6 to 6
- pole_rates: float32 [8, 4096], P(None, 'chan'), may hold values from 0 to 1, as said below
- pole_weights: float32 [8, 4096], P(None, 'chan'), may hold values from -4 to 4
- skip_gain: float32 [4096], P('chan'), may hold values from -1 to 1
- query_rows: bfloat16 [8192, 4096], P('seq', 'chan'), may hold values from -6 to 6
- key_rows: bfloat16 [8192, 4096], P('seq', 'chan'), may hold values from -6 to 6
Outputs:
- mixed: bfloat16 [8192, 4096], P('seq', 'chan')
Inputs may be any that keep to these rules, and one draw needn't show every extreme that they name: `pole_rates`: each rate is positive and at most 1/30.
All inputs are finite; a program needn't handle non-finite values.
Results may differ from a plain program's by a relative error of at most 0.0065.
Values may be sent and summed in bfloat16 or wider, within the bound.
A program may use at most 128 MiB of HBM per device.

v0:
```python
import math
import jax
import jax.numpy as jnp
from jax import lax
from jax.sharding import PartitionSpec as P

HD = 128


def prefix(part, axis, combine, identity):
    place = lax.axis_index(axis)
    gathered = jax.tree.map(lambda a: lax.all_gather(a, axis), part)
    state = jax.tree.map(lambda a, e: jnp.zeros_like(a) + jnp.asarray(e, a.dtype), part, identity)

    def one(turn, state):
        return combine(
            state, jax.tree.map(lambda a: lax.dynamic_index_in_dim(a, turn, 0, False), gathered)
        )

    return lax.fori_loop(0, place, one, state)


def block_update(carried, queries, query_pos, key_part, value_part, key_start, score_scale):
    run_max, run_sum, run_acc = carried
    heads_here = run_max.shape[0]
    key_count = key_part.shape[0]
    query_heads = queries.reshape(queries.shape[0], heads_here, -1)
    key_heads = key_part.reshape(key_count, heads_here, -1)
    value_heads = value_part.reshape(key_count, heads_here, -1)
    scores = (
        jnp.einsum("qhd,khd->hqk", query_heads, key_heads, preferred_element_type=jnp.float32)
        * score_scale
    )
    key_pos = key_start + jnp.arange(key_count, dtype=jnp.int32)
    visible = key_pos[None, None, :] <= query_pos[None, :, None]
    scores = jnp.where(visible, scores, -1e30)
    new_max = jnp.maximum(run_max, jnp.max(scores, axis=2))
    rescale = jnp.exp(run_max - new_max)
    expo = jnp.where(visible, jnp.exp(scores - new_max[:, :, None]), 0.0)
    new_sum = run_sum * rescale + jnp.sum(expo, axis=2)
    new_acc = run_acc * rescale[:, :, None] + jnp.einsum(
        "hqk,khd->hqd", expo.astype(jnp.bfloat16), value_heads, preferred_element_type=jnp.float32
    )
    return (new_max, new_sum, new_acc)


def fold_keys(carried, queries, query_pos, pieces, score_scale):
    key_piece, value_piece = pieces
    count_rows = key_piece.shape[0]
    step_rows = math.gcd(count_rows, 1024)

    def one_step(step_index, current):
        sub_start = step_index * step_rows
        key_part = lax.dynamic_slice_in_dim(key_piece, sub_start, step_rows, 0)
        value_part = lax.dynamic_slice_in_dim(value_piece, sub_start, step_rows, 0)
        return block_update(
            current, queries, query_pos, key_part, value_part, sub_start, score_scale
        )

    return lax.fori_loop(0, count_rows // step_rows, one_step, carried)


def finish(carried):
    run_max, run_sum, run_acc = carried
    normed = run_acc / run_sum[:, :, None]
    heads_here, rows_here, depth = normed.shape
    return (
        jnp.transpose(normed, (1, 0, 2)).reshape(rows_here, heads_here * depth).astype(jnp.bfloat16)
    )


def local(
    gate_outer, gate_inner, value_in, pole_rates, pole_weights, skip_gain, query_rows, key_rows
):
    tok_rows, width = gate_outer.shape
    poles_here = pole_rates.shape[0]
    seq_index = lax.axis_index("seq")
    chan_count = lax.axis_size("chan")
    gated = gate_inner.astype(jnp.float32) * value_in.astype(jnp.float32)
    offsets = jnp.arange(tok_rows, dtype=jnp.float32)
    growth = jnp.exp(offsets[:, None, None] * pole_rates[None, :, :])
    weighted = growth * gated[:, None, :]
    lower = (jnp.arange(tok_rows)[:, None] >= jnp.arange(tok_rows)[None, :]).astype(jnp.float32)
    running = jnp.dot(
        lower, weighted.reshape(tok_rows, poles_here * width), precision=lax.Precision.HIGHEST
    )
    running = running.reshape(tok_rows, poles_here, width)
    block_span = jnp.float32(tok_rows)
    summary = running[-1] * jnp.exp(-(block_span - 1.0) * pole_rates)

    def chain_states(earlier, later):
        fade = jnp.exp(-block_span * later[1] * pole_rates)
        return (later[0] + fade * earlier[0], earlier[1] + later[1])

    identity = (jnp.zeros_like(summary), jnp.zeros((1, 1), jnp.float32))
    carry_in, block_count = prefix(
        (summary, jnp.ones((1, 1), jnp.float32)), "seq", chain_states, identity
    )
    decayed = jnp.exp(-offsets[:, None, None] * pole_rates[None, :, :])
    modal = decayed * (running + (jnp.exp(-pole_rates) * carry_in)[None, :, :])
    filtered = jnp.sum(modal * (pole_weights * jnp.sqrt(pole_rates))[None, :, :], axis=1)
    conv_out = gate_outer.astype(jnp.float32) * (filtered + skip_gain[None, :] * gated)
    local_squares = jnp.sum(conv_out * conv_out, axis=1)
    total_squares = lax.psum(local_squares, "chan")
    mean_square = total_squares / (width * chan_count)
    values = (conv_out * lax.rsqrt(mean_square[:, None] + 1e-06)).astype(jnp.bfloat16)
    score_scale = HD ** (-0.5)
    heads_here = width // HD
    my_start = seq_index * tok_rows
    all_pos = my_start + jnp.arange(tok_rows, dtype=jnp.int32)
    final_state = fold_keys(
        (
            jnp.full((heads_here, tok_rows), -1e30, jnp.float32),
            jnp.zeros((heads_here, tok_rows), jnp.float32),
            jnp.zeros((heads_here, tok_rows, HD), jnp.float32),
        ),
        query_rows,
        all_pos,
        (
            lax.all_gather(key_rows, "seq", axis=0, tiled=True),
            lax.all_gather(values, "seq", axis=0, tiled=True),
        ),
        score_scale,
    )
    mixed = finish(final_state)
    return mixed


def solution(mesh):
    in_specs = (
        P("seq", "chan"),
        P("seq", "chan"),
        P("seq", "chan"),
        P(None, "chan"),
        P(None, "chan"),
        P("chan"),
        P("seq", "chan"),
        P("seq", "chan"),
    )
    out_specs = P("seq", "chan")
    return jax.shard_map(local, mesh=mesh, in_specs=in_specs, out_specs=out_specs, check_vma=False)
```

profile of v0, /device:TPU:1, one launch (start us, length us, event | category | flops | bytes accessed | tf_op | source)
XLA Modules:
  0.0 426.7 jit_solution(17308309685470993890)
XLA Ops:
  7.3 1.0 convert_multiply_fusion
  8.5 1.6 copy.36
  10.2 1.6 fusion.21
  13.4 3.0 copy.37
  16.4 1.3 dynamic-slice
  18.5 130.3 %all-reduce = f32[64]{0:T(128)S(1)} all-reduce(f32[64]{0:T(128)S(1)} %dynamic-update-slice), channel_id=1, replica_groups=mesh['seq'=64,'chan'=8] {'seq'}, use_global_device_ids=true, to_apply=%add | all-reduce | flops 64 | bytes 512
  148.8 2.0 while.30
  149.5 1.4 bitcast_add_fusion.3
  150.9 2.6 fusion.20
  153.7 16.0 %psum.7 = f32[128]{0:T(128)S(1)} all-reduce(f32[128]{0:T(128)S(1)} %multiply_reduce_fusion), channel_id=1, replica_groups=mesh['seq'=64,'chan'=8] {'chan'}, use_global_device_ids=true, to_apply=%region_4.5 | all-reduce | flops 128 | bytes 1024 | tf_op jit(solution)/shard_map/psum | solution.py:104
  170.5 21.5 %all-gather.5.cloned.1.call-done = bf16[8192,512]{0,1:T(8,128)(2,1)} async-done(((bf16[128,512]{0,1:T(8,128)(2,1)}), bf16[8192,512]{0,1:T(8,128)(2,1)}) %all-gather.5.cloned.1.call-update) | async-done | bytes 8388624 | tf_op jit(solution)/shard_map/all_gather | solution.py:120
  192.0 183.1 %all-gather.7.cloned.1.call-done = bf16[8192,512]{1,0:T(8,128)(2,1)} async-done(((bf16[128,512]{1,0:T(8,128)(2,1)}), bf16[8192,512]{1,0:T(8,128)(2,1)}) %all-gather.7.cloned.1.call-update) | async-done | bytes 8388624 | tf_op jit(solution)/shard_map/all_gather | solution.py:121
  375.1 44.3 %while.31 = (s32[]{:T(128)}, f32[4,128]{1,0:T(4,128)S(1)}, f32[4,128]{1,0:T(4,128)S(1)}, f32[4,128,128]{2,1,0:T(8,128)S(1)}, bf16[8192,512]{0,1:T(8,128)(2,1)}, ...) while((s32[]{:T(128)}, f32[4,128]{1,0:T(4,128)S(1)}, ...), condition=%wide.region_8.9_spmd.clone, body=%wide.region_5.8_spmd.clone.sunk | while | flops 275582592 | bytes 15901895 | solution.py:60
  375.3 1.3 constant_dynamic-slice_fusion.6
  377.2 1.3 constant_dynamic-slice_fusion.5
  380.9 1.3 constant_dynamic-slice_fusion.6
  382.7 1.3 constant_dynamic-slice_fusion.5
  385.2 0.9 convolution_add_fusion.2
  386.4 1.3 constant_dynamic-slice_fusion.6
  388.2 1.3 constant_dynamic-slice_fusion.5
  391.9 1.3 constant_dynamic-slice_fusion.6
  393.8 1.3 constant_dynamic-slice_fusion.5
  396.3 0.9 convolution_add_fusion.2
  397.5 1.3 constant_dynamic-slice_fusion.6
  399.3 1.3 constant_dynamic-slice_fusion.5
  403.0 1.3 constant_dynamic-slice_fusion.6
  404.9 1.3 constant_dynamic-slice_fusion.5
  407.4 0.9 convolution_add_fusion.2
  408.5 1.3 constant_dynamic-slice_fusion.6
  410.4 1.3 constant_dynamic-slice_fusion.5
  414.1 1.3 constant_dynamic-slice_fusion.6
  415.9 1.3 constant_dynamic-slice_fusion.5
  (119 shorter events, 25.8 us)
Async XLA Ops:
  6.5 142.3 %all-gather.9.cloned.1.call-start = ((), (), s32[]{:S(2)}) async-start(), calls=%async_computation.2 | async-start | bytes 1064960 | tf_op jit(solution)/shard_map/all_gather | solution.py:12
  10.2 1.7 copy-start.1
  10.2 2.3 copy-start.5
  12.5 179.6 %all-gather.5.cloned.1.call-start = ((), (), s32[]{:S(2)}) async-start(), calls=%async_computation | async-start | bytes 8519680 | tf_op jit(solution)/shard_map/all_gather | solution.py:120
  13.3 361.8 %all-gather.7.cloned.1.call-start = ((), (), s32[]{:S(2)}) async-start(), calls=%async_computation.1 | async-start | bytes 8519680 | tf_op jit(solution)/shard_map/all_gather | solution.py:121
  13.4 137.5 %copy-start.6 = (f32[8,512]{1,0:T(8,128)S(1)}, f32[8,512]{1,0:T(8,128)}, u32[]{:S(2)}) copy-start(f32[8,512]{1,0:T(8,128)} %param.16) | copy-start | bytes 49156
  16.4 137.1 %copy-start.2 = (bf16[128,512]{1,0:T(8,128)(2,1)S(1)}, bf16[128,512]{1,0:T(8,128)(2,1)}, u32[]{:S(2)}) copy-start(bf16[128,512]{1,0:T(8,128)(2,1)} %param.14) | copy-start | bytes 393220
  16.4 137.1 %copy-start.3 = (bf16[128,512]{1,0:T(8,128)(2,1)S(1)}, bf16[128,512]{1,0:T(8,128)(2,1)}, u32[]{:S(2)}) copy-start(bf16[128,512]{1,0:T(8,128)(2,1)} %param.13) | copy-start | bytes 393220
  16.4 137.1 %copy-start.4 = (bf16[128,512]{1,0:T(8,128)(2,1)S(1)}, bf16[128,512]{1,0:T(8,128)(2,1)}, u32[]{:S(2)}) copy-start(bf16[128,512]{1,0:T(8,128)(2,1)} %param.12) | copy-start | bytes 393220
  16.4 137.1 %copy-start.7 = (f32[512]{0:T(512)S(1)}, f32[512]{0:T(512)}, u32[]{:S(2)}) copy-start(f32[512]{0:T(512)} %param.17) | copy-start | bytes 6148
  150.9 224.2 %copy-start = (bf16[128,512]{1,0:T(8,128)(2,1)S(1)}, bf16[128,512]{1,0:T(8,128)(2,1)}, u32[]{:S(2)}) copy-start(bf16[128,512]{1,0:T(8,128)(2,1)} %param.18) | copy-start | bytes 393220
Sparse Core Ops, SparseCore 0:
  12.6 87.8 all-gather.8
  103.6 88.3 all-gather.4
  195.4 179.6 all-gather.6
where the time goes:
time: 433 us; the launch traced here: 427 us
  waiting for transfers between devices  205 us (47%)
  blocking collectives  146 us (34%)
  local copies, waits for them, and re-layouts  33.7 us (8%)
  other arithmetic  14.1 us (3%)
  matrix products  13.9 us (3%)
  between operations  13.3 us (3%)
    all_gather x1, waiting for transfers between devices, local(): lax.all_gather(values, 'seq', axis=0, tiled=True)  183 us
    unnamed x1, blocking collectives  130 us
    all_gather x1, waiting for transfers between devices, local(): lax.all_gather(key_rows, 'seq', axis=0, tiled=True)  21.5 us
    psum x1, blocking collectives, local(): total_squares = lax.psum(local_squares, 'chan')  16 us
    dynamic_slice x16, local copies, waits for them, and re-layouts, one_step(): value_part = lax.dynamic_slice_in_dim(value_piece, sub_start, step_rows, 0)  14.7 us
    dynamic_slice x8, local copies, waits for them, and re-layouts, one_step(): key_part = lax.dynamic_slice_in_dim(key_piece, sub_start, step_rows, 0)  10.4 us
  transfers between devices with their start and end apart: 3, of which 2 were waited for; matrix products, arithmetic and copies ran while one was open for 3% of the time, Pallas kernels for 0%

commit v1 on v0

--- a/solution.py
+++ b/solution.py
@@ -72,6 +72,10 @@
 def local(
     gate_outer, gate_inner, value_in, pole_rates, pole_weights, skip_gain, query_rows, key_rows
 ):
+
+    def arrays_draw(x_in):
+        return jnp.sum(jax.lax.all_gather(x_in, "chan"), axis=0)
+
     tok_rows, width = gate_outer.shape
     poles_here = pole_rates.shape[0]
     seq_index = lax.axis_index("seq")
@@ -101,7 +105,7 @@
     filtered = jnp.sum(modal * (pole_weights * jnp.sqrt(pole_rates))[None, :, :], axis=1)
     conv_out = gate_outer.astype(jnp.float32) * (filtered + skip_gain[None, :] * gated)
     local_squares = jnp.sum(conv_out * conv_out, axis=1)
-    total_squares = lax.psum(local_squares, "chan")
+    total_squares = arrays_draw(local_squares)
     mean_square = total_squares / (width * chan_count)
     values = (conv_out * lax.rsqrt(mean_square[:, None] + 1e-06)).astype(jnp.bfloat16)
     score_scale = HD ** (-0.5)

time: 433 us -> 433 us (level)
    psum x1 -> x0, blocking collectives: 16 us -> none  [local(): total_squares = lax.psum(local_squares, 'chan')]
    all_gather x0 -> x1, blocking collectives: none -> 15.1 us  [arrays_draw(): return jnp.sum(jax.lax.all_gather(x_in, 'chan'), axis=0)]
where the time goes in v1:
time: 433 us; the launch traced here: 426 us
  waiting for transfers between devices  205 us (47%)
  blocking collectives  145 us (33%)
  local copies, waits for them, and re-layouts  33.7 us (8%)
  other arithmetic  14.1 us (3%)
  matrix products  13.9 us (3%)
  between operations  13.3 us (3%)
    all_gather x1, waiting for transfers between devices, local(): lax.all_gather(values, 'seq', axis=0, tiled=True)  182 us
    unnamed x1, blocking collectives  130 us
    all_gather x1, waiting for transfers between devices, local(): lax.all_gather(key_rows, 'seq', axis=0, tiled=True)  22.6 us
    all_gather x1, blocking collectives, arrays_draw(): return jnp.sum(jax.lax.all_gather(x_in, 'chan'), axis=0)  15.1 us
    dynamic_slice x16, local copies, waits for them, and re-layouts, one_step(): value_part = lax.dynamic_slice_in_dim(value_piece, sub_start, step_rows, 0)  14.7 us
    dynamic_slice x8, local copies, waits for them, and re-layouts, one_step(): key_part = lax.dynamic_slice_in_dim(key_piece, sub_start, step_rows, 0)  10.4 us
  transfers between devices with their start and end apart: 3, of which 2 were waited for; matrix products, arithmetic and copies ran while one was open for 3% of the time, Pallas kernels for 0%

profile of v1, /device:TPU:1, one launch (start us, length us, event | category | flops | bytes accessed | tf_op | source)
XLA Modules:
  0.0 425.9 jit_solution(10612231366201208313)
XLA Ops:
  7.3 1.0 convert_multiply_fusion
  8.5 1.6 copy.36
  10.2 1.6 fusion.21
  13.4 3.0 copy.37
  16.4 1.3 dynamic-slice
  18.5 130.3 %all-reduce = f32[64]{0:T(128)S(1)} all-reduce(f32[64]{0:T(128)S(1)} %dynamic-update-slice), channel_id=1, replica_groups=mesh['seq'=64,'chan'=8] {'seq'}, use_global_device_ids=true, to_apply=%add | all-reduce | flops 64 | bytes 512
  148.8 2.0 while.30
  149.5 1.4 bitcast_add_fusion.3
  150.9 2.6 fusion.20
  153.7 15.1 %all-gather.2 = f32[8,1,128]{2,1,0:T(1,128)S(1)} all-gather(f32[1,1,128]{2,1,0:T(1,128)S(1)} %bitcast.80), channel_id=3, replica_groups=mesh['seq'=64,'chan'=8] {'chan'}, dimensions={0}, use_global_device_ids=true | all-gather | bytes 4608 | tf_op jit(solution)/shard_map/all_gather | solution.py:77
  169.6 22.6 %all-gather.7.cloned.1.call-done = bf16[8192,512]{0,1:T(8,128)(2,1)} async-done(((bf16[128,512]{0,1:T(8,128)(2,1)}), bf16[8192,512]{0,1:T(8,128)(2,1)}) %all-gather.7.cloned.1.call-update) | async-done | bytes 8388624 | tf_op jit(solution)/shard_map/all_gather | solution.py:124
  192.2 182.0 %all-gather.9.cloned.1.call-done = bf16[8192,512]{1,0:T(8,128)(2,1)} async-done(((bf16[128,512]{1,0:T(8,128)(2,1)}), bf16[8192,512]{1,0:T(8,128)(2,1)}) %all-gather.9.cloned.1.call-update) | async-done | bytes 8388624 | tf_op jit(solution)/shard_map/all_gather | solution.py:125
  374.3 44.3 %while.31 = (s32[]{:T(128)}, f32[4,128]{1,0:T(4,128)S(1)}, f32[4,128]{1,0:T(4,128)S(1)}, f32[4,128,128]{2,1,0:T(8,128)S(1)}, bf16[8192,512]{0,1:T(8,128)(2,1)}, ...) while((s32[]{:T(128)}, f32[4,128]{1,0:T(4,128)S(1)}, ...), condition=%wide.region_8.9_spmd.clone, body=%wide.region_5.8_spmd.clone.sunk | while | flops 275582592 | bytes 15901895 | solution.py:60
  374.5 1.3 constant_dynamic-slice_fusion.6
  376.3 1.3 constant_dynamic-slice_fusion.5
  378.8 0.9 convolution_add_fusion.2
  380.0 1.3 constant_dynamic-slice_fusion.6
  381.9 1.3 constant_dynamic-slice_fusion.5
  384.4 0.9 convolution_add_fusion.2
  385.6 1.3 constant_dynamic-slice_fusion.6
  387.4 1.3 constant_dynamic-slice_fusion.5
  391.1 1.3 constant_dynamic-slice_fusion.6
  392.9 1.3 constant_dynamic-slice_fusion.5
  395.4 0.9 convolution_add_fusion.2
  396.6 1.3 constant_dynamic-slice_fusion.6
  398.5 1.3 constant_dynamic-slice_fusion.5
  402.2 1.3 constant_dynamic-slice_fusion.6
  404.0 1.3 constant_dynamic-slice_fusion.5
  407.7 1.3 constant_dynamic-slice_fusion.6
  409.6 1.3 constant_dynamic-slice_fusion.5
  413.2 1.3 constant_dynamic-slice_fusion.6
  415.1 1.3 constant_dynamic-slice_fusion.5
  (120 shorter events, 25.8 us)
Async XLA Ops:
  6.5 142.3 %all-gather.11.cloned.1.call-start = ((), (), s32[]{:S(2)}) async-start(), calls=%async_computation.2 | async-start | bytes 1064960 | tf_op jit(solution)/shard_map/all_gather | solution.py:12
  10.2 1.7 copy-start.1
  10.2 2.3 copy-start.5
  12.5 179.7 %all-gather.7.cloned.1.call-start = ((), (), s32[]{:S(2)}) async-start(), calls=%async_computation | async-start | bytes 8519680 | tf_op jit(solution)/shard_map/all_gather | solution.py:124
  13.3 360.9 %all-gather.9.cloned.1.call-start = ((), (), s32[]{:S(2)}) async-start(), calls=%async_computation.1 | async-start | bytes 8519680 | tf_op jit(solution)/shard_map/all_gather | solution.py:125
  13.4 137.5 %copy-start.6 = (f32[8,512]{1,0:T(8,128)S(1)}, f32[8,512]{1,0:T(8,128)}, u32[]{:S(2)}) copy-start(f32[8,512]{1,0:T(8,128)} %param.16) | copy-start | bytes 49156
  16.4 137.1 %copy-start.2 = (bf16[128,512]{1,0:T(8,128)(2,1)S(1)}, bf16[128,512]{1,0:T(8,128)(2,1)}, u32[]{:S(2)}) copy-start(bf16[128,512]{1,0:T(8,128)(2,1)} %param.14) | copy-start | bytes 393220
  16.4 137.1 %copy-start.3 = (bf16[128,512]{1,0:T(8,128)(2,1)S(1)}, bf16[128,512]{1,0:T(8,128)(2,1)}, u32[]{:S(2)}) copy-start(bf16[128,512]{1,0:T(8,128)(2,1)} %param.13) | copy-start | bytes 393220
  16.4 137.1 %copy-start.4 = (bf16[128,512]{1,0:T(8,128)(2,1)S(1)}, bf16[128,512]{1,0:T(8,128)(2,1)}, u32[]{:S(2)}) copy-start(bf16[128,512]{1,0:T(8,128)(2,1)} %param.12) | copy-start | bytes 393220
  16.4 137.1 %copy-start.7 = (f32[512]{0:T(512)S(1)}, f32[512]{0:T(512)}, u32[]{:S(2)}) copy-start(f32[512]{0:T(512)} %param.17) | copy-start | bytes 6148
  150.9 223.4 %copy-start = (bf16[128,512]{1,0:T(8,128)(2,1)S(1)}, bf16[128,512]{1,0:T(8,128)(2,1)}, u32[]{:S(2)}) copy-start(bf16[128,512]{1,0:T(8,128)(2,1)} %param.18) | copy-start | bytes 393220
Sparse Core Ops, SparseCore 0:
  12.6 87.8 all-gather.10
  103.6 88.5 all-gather.6
  195.6 178.6 all-gather.8
